TPU v7x, 32 devices: a whole 2x2x4 slice. The times are simulated.
32 devices in a mesh: seqmaj: 4 (over y, x), seqmin: 8 (over z, core).
Axes of the slice: x: 2, y: 2, z: 4, core: 2. Of those that a mesh axis runs over, the one named last changes fastest.
Arguments:
- q_first: bfloat16 [4096, 2048], P(('seqmaj', 'seqmin')), may hold values from -6 to 6
- k_first: bfloat16 [4096, 2048], P(('seqmaj', 'seqmin')), may hold values from -6 to 6
- v_first: bfloat16 [4096, 2048], P(('seqmaj', 'seqmin')), may hold values from -6 to 6
- mr_filter: bfloat16 [128, 2048], replicated, may hold values from -0.5 to 0.5
- mr_skip: float32 [2048], replicated, may hold values from -4 to 4
- value_weight: bfloat16 [2048, 2048], replicated, may hold values from -0.125 to 0.125
- q_second: bfloat16 [4096, 2048], P(('seqmaj', 'seqmin')), may hold values from -6 to 6
- k_second: bfloat16 [4096, 2048], P(('seqmaj', 'seqmin')), may hold values from -6 to 6
- li_residue: float32 [16, 2048], replicated, may hold values from -3 to 3
- li_rate: float32 [16, 2048], replicated, may hold values from 0.00012207031 to 0.033333335
- li_skip: float32 [2048], replicated, may hold values from -4 to 4
- out_second: bfloat16 [2048, 2048], replicated, may hold values from -0.0625 to 0.0625
Outputs:
- mixed: bfloat16 [4096, 2048], P(('seqmaj', 'seqmin'))
All inputs are finite; a program needn't handle non-finite values.
Results may differ from a plain program's by a relative error of at most 0.015.
Values may be sent and summed in bfloat16 or wider, within the bound.
A program may use at most 128 MiB of HBM per device.

v0:
```python
import math

import jax
import jax.numpy as jnp
from jax import lax
from jax.sharding import PartitionSpec as P

highest = lax.Precision.HIGHEST


def shortened(x):
    return jax.tree.map(lambda a: a.astype(jnp.bfloat16) if a.dtype == jnp.float32 else a, x)


def passed_along(block, axis, distance):
    devices = range(lax.axis_size(axis))
    route = [(i - distance, i) for i in devices if i - distance in devices]
    return lax.ppermute(block, axis, route)


def tap_convolution(window, filter_taps):
    flipped = filter_taps[::-1][:, None, :]
    result = lax.conv_general_dilated(
        window[None],
        flipped,
        (1,),
        "VALID",
        dimension_numbers=("NWC", "WIO", "NWC"),
        feature_group_count=window.shape[1],
        preferred_element_type=jnp.float32,
    )
    return result[0]


def phase_table(left_index, right_index, length, sign_value):
    product = left_index[:, None] * right_index[None, :] % length
    angle = 2.0 * math.pi / length * product.astype(jnp.float32)
    return (jnp.cos(angle), sign_value * jnp.sin(angle))


def complex_product(table_re, table_im, data_re, data_im, pattern):
    real_part = jnp.einsum(pattern, table_re, data_re, precision=highest) - jnp.einsum(
        pattern, table_im, data_im, precision=highest
    )
    imag_part = jnp.einsum(pattern, table_re, data_im, precision=highest) + jnp.einsum(
        pattern, table_im, data_re, precision=highest
    )
    return (real_part, imag_part)


def forward_outer(columns, positions, total_size):
    devices = columns.shape[0]
    slice_rows = columns.shape[1]
    channels = columns.shape[2]
    outer_size = 2 * devices
    outer_index = jnp.arange(outer_size, dtype=jnp.int32)
    block_index = jnp.arange(devices, dtype=jnp.int32)
    cosines, signed_sines = phase_table(outer_index, block_index, outer_size, -1.0)
    flattened = columns.reshape(devices, slice_rows * channels)
    part_re = jnp.dot(cosines, flattened, precision=highest).reshape(
        outer_size, slice_rows, channels
    )
    part_im = jnp.dot(signed_sines, flattened, precision=highest).reshape(
        outer_size, slice_rows, channels
    )
    twist_re, twist_im = phase_table(outer_index, positions, total_size, -1.0)
    twist_re = twist_re[:, :, None]
    twist_im = twist_im[:, :, None]
    return jnp.stack(
        [part_re * twist_re - part_im * twist_im, part_re * twist_im + part_im * twist_re]
    )


def local_forward(data_re, data_im, factor):
    count = data_re.shape[0]
    row_count = data_re.shape[1]
    channels = data_re.shape[2]
    inner_size = row_count // factor
    block_re = data_re.reshape(count, factor, inner_size, channels)
    block_im = data_im.reshape(count, factor, inner_size, channels)
    low_digits = jnp.arange(factor, dtype=jnp.int32)
    high_digits = jnp.arange(inner_size, dtype=jnp.int32)
    table_re, table_im = phase_table(low_digits, low_digits, factor, -1.0)
    section_re, section_im = complex_product(
        table_re, table_im, block_re, block_im, "ca,kabw->kcbw"
    )
    twist_re, twist_im = phase_table(low_digits, high_digits, row_count, -1.0)
    twist_re = twist_re[None, :, :, None]
    twist_im = twist_im[None, :, :, None]
    mixed_re = section_re * twist_re - section_im * twist_im
    mixed_im = section_re * twist_im + section_im * twist_re
    table_re, table_im = phase_table(high_digits, high_digits, inner_size, -1.0)
    return complex_product(table_re, table_im, mixed_re, mixed_im, "eb,kcbw->kcew")


def local_inverse(data_re, data_im, factor):
    count = data_re.shape[0]
    inner_size = data_re.shape[2]
    channels = data_re.shape[3]
    row_count = factor * inner_size
    low_digits = jnp.arange(factor, dtype=jnp.int32)
    high_digits = jnp.arange(inner_size, dtype=jnp.int32)
    table_re, table_im = phase_table(high_digits, high_digits, inner_size, 1.0)
    section_re, section_im = complex_product(table_re, table_im, data_re, data_im, "be,kcew->kcbw")
    twist_re, twist_im = phase_table(low_digits, high_digits, row_count, 1.0)
    twist_re = twist_re[None, :, :, None]
    twist_im = twist_im[None, :, :, None]
    mixed_re = section_re * twist_re - section_im * twist_im
    mixed_im = section_re * twist_im + section_im * twist_re
    table_re, table_im = phase_table(low_digits, low_digits, factor, 1.0)
    result_re, result_im = complex_product(table_re, table_im, mixed_re, mixed_im, "ac,kcbw->kabw")
    return (
        result_re.reshape(count, row_count, channels),
        result_im.reshape(count, row_count, channels),
    )


def inverse_outer(returned, total_size):
    outer_size = returned.shape[1]
    slice_rows = returned.shape[2]
    channels = returned.shape[3]
    devices = outer_size // 2
    cosines, signed_sines = phase_table(
        jnp.arange(devices, dtype=jnp.int32),
        jnp.arange(outer_size, dtype=jnp.int32),
        outer_size,
        1.0,
    )
    flat_re = returned[0].reshape(outer_size, slice_rows * channels)
    flat_im = returned[1].reshape(outer_size, slice_rows * channels)
    values = jnp.dot(cosines, flat_re, precision=highest) - jnp.dot(
        signed_sines, flat_im, precision=highest
    )
    return (values / total_size).reshape(devices, slice_rows, channels)


def long_convolution(signal, residue, rate):
    row_count = signal.shape[0]
    channels = signal.shape[1]
    major_count = lax.axis_size("seqmaj")
    minor_count = lax.axis_size("seqmin")
    devices = major_count * minor_count
    slice_rows = row_count // devices
    outer_size = 2 * devices
    total_size = outer_size * row_count
    factor = 32
    major_index = lax.axis_index("seqmaj")
    minor_index = lax.axis_index("seqmin")
    device = major_index * minor_count + minor_index
    slice_offsets = jnp.arange(slice_rows, dtype=jnp.int32)
    columns = lax.all_to_all(
        signal[None], ("seqmaj", "seqmin"), split_axis=1, concat_axis=0, tiled=True
    )
    positions = device * slice_rows + slice_offsets
    spread = forward_outer(columns.astype(jnp.float32), positions, total_size)
    gathered = lax.all_to_all(
        shortened(spread), ("seqmaj", "seqmin"), split_axis=1, concat_axis=2, tiled=True
    ).astype(spread.dtype)
    data_re, data_im = local_forward(gathered[0], gathered[1], factor)
    own_outer = device * 2 + jnp.arange(2, dtype=jnp.int32)
    times = (device * row_count + jnp.arange(row_count, dtype=jnp.int32)).astype(jnp.float32)
    weight = residue * jnp.sqrt(rate)
    filter_values = jnp.sum(
        weight[:, None, :] * jnp.exp(-rate[:, None, :] * times[None, :, None]), axis=0
    )
    filter_columns = lax.all_to_all(
        filter_values[None].astype(jnp.bfloat16),
        ("seqmaj", "seqmin"),
        split_axis=1,
        concat_axis=0,
        tiled=True,
    ).astype(jnp.float32)
    filter_spread = forward_outer(filter_columns, device * slice_rows + slice_offsets, total_size)
    filter_gathered = lax.all_to_all(
        shortened(filter_spread), ("seqmaj", "seqmin"), split_axis=1, concat_axis=2, tiled=True
    ).astype(filter_spread.dtype)
    filter_re, filter_im = local_forward(filter_gathered[0], filter_gathered[1], factor)
    product_re = data_re * filter_re - data_im * filter_im
    product_im = data_re * filter_im + data_im * filter_re
    back_re, back_im = local_inverse(product_re, product_im, factor)
    twist_re, twist_im = phase_table(
        own_outer, jnp.arange(row_count, dtype=jnp.int32), total_size, 1.0
    )
    twist_re = twist_re[:, :, None]
    twist_im = twist_im[:, :, None]
    turned = jnp.stack(
        [back_re * twist_re - back_im * twist_im, back_re * twist_im + back_im * twist_re]
    )
    returned = lax.all_to_all(
        shortened(turned), ("seqmaj", "seqmin"), split_axis=2, concat_axis=1, tiled=True
    ).astype(turned.dtype)
    values = inverse_outer(returned, total_size)
    rows_back = lax.all_to_all(
        shortened(values), ("seqmaj", "seqmin"), split_axis=0, concat_axis=1, tiled=True
    ).astype(values.dtype)
    return rows_back.reshape(row_count, channels)


def local(
    q_first,
    k_first,
    v_first,
    mr_filter,
    mr_skip,
    value_weight,
    q_second,
    k_second,
    li_residue,
    li_rate,
    li_skip,
    out_second,
):
    row_count = q_first.shape[0]
    tap_count = mr_filter.shape[0]
    gated_first = (k_first.astype(jnp.float32) * v_first.astype(jnp.float32)).astype(jnp.bfloat16)
    border = passed_along(gated_first[row_count - (tap_count - 1) :], ("seqmaj", "seqmin"), 1)
    window = jnp.concatenate([border, gated_first], axis=0)
    short_conv = tap_convolution(window, mr_filter)
    first_act = (
        q_first.astype(jnp.float32)
        * (short_conv + mr_skip[None, :] * gated_first.astype(jnp.float32))
    ).astype(jnp.bfloat16)
    v_second = jnp.dot(first_act, value_weight, preferred_element_type=jnp.float32).astype(
        jnp.bfloat16
    )
    gated_second = (k_second.astype(jnp.float32) * v_second.astype(jnp.float32)).astype(
        jnp.bfloat16
    )
    long_conv = long_convolution(gated_second, li_residue, li_rate)
    second_act = (
        q_second.astype(jnp.float32)
        * (long_conv + li_skip[None, :] * gated_second.astype(jnp.float32))
    ).astype(jnp.bfloat16)
    return jnp.dot(second_act, out_second, preferred_element_type=jnp.float32).astype(jnp.bfloat16)


def solution(mesh):
    in_specs = (
        P(("seqmaj", "seqmin"), None),
        P(("seqmaj", "seqmin"), None),
        P(("seqmaj", "seqmin"), None),
        P(),
        P(),
        P(),
        P(("seqmaj", "seqmin"), None),
        P(("seqmaj", "seqmin"), None),
        P(),
        P(),
        P(),
        P(),
    )
    out_specs = P(("seqmaj", "seqmin"), None)
    return jax.shard_map(local, mesh=mesh, in_specs=in_specs, out_specs=out_specs, check_vma=False)
```

profile of v0, /device:TPU:0, one launch (start us, length us, event | category | flops | bytes accessed | tf_op | source)
XLA Modules:
  0.0 376.8 jit_solution(13869307151583801568)
XLA Ops:
  13.7 6.6 %all-to-all-start.2 = ((bf16[32,2,4096]{2,1,0:T(2,128)(2,1)}), bf16[32,2,4096]{2,1,0:T(2,128)(2,1)S(1)}, u32[]{:S(2)}, u32[]{:S(2)}) async-start(bf16[32,2,4096]{2,1,0:T(2,128)(2,1)} %reshape.296), calls=%async_computation.2 | async-start | bytes 1048576 | tf_op jit(solution)/shard_map/all_to_all | solution.py:166
  20.2 5.1 %rev.3 = bf16[128,2048]{1,0:T(8,128)(2,1)} reverse(bf16[128,2048]{1,0:T(8,128)(2,1)S(1)} %copy-done.7), dimensions={0} | reverse | bytes 1048576 | tf_op jit(solution)/shard_map/rev | solution.py:22
  26.8 14.9 %fusion.21 = f32[1,128,2048]{2,0,1:T(1,128)S(1)} fusion(bf16[1,255,2048]{2,1,0:T(8,128)(2,1)S(1)} %maximum_bitcast_fusion, bf16[128,1,2048]{2,0,1:T(8,128)(2,1)S(1)} %bitcast.243), kind=kOutput, calls=%fused_computation.59 | convolution fusion | flops 67108864 | bytes 2617344 | tf_op jit(solution)/shard_map/conv_general_dilated | solution.py:23
  49.1 6.3 %all-to-all-start = ((bf16[32,2,4096]{2,1,0:T(2,128)(2,1)}), bf16[32,2,4096]{2,1,0:T(2,128)(2,1)}, u32[]{:S(2)}, u32[]{:S(2)}) async-start(bf16[32,2,4096]{2,1,0:T(2,128)(2,1)} %reshape.294), calls=%async_computation | async-start | bytes 1048576 | tf_op jit(solution)/shard_map/all_to_all | solution.py:151
  63.1 8.7 %all-to-all-done = bf16[32,2,4096]{2,1,0:T(2,128)(2,1)} async-done(((bf16[32,2,4096]{2,1,0:T(2,128)(2,1)}), bf16[32,2,4096]{2,1,0:T(2,128)(2,1)}, u32[]{:S(2)}, u32[]{:S(2)}) %all-to-all-start) | async-done | bytes 524320 | tf_op jit(solution)/shard_map/all_to_all | solution.py:151
  71.7 4.9 %reshape.295 = bf16[128,1,2048]{2,1,0:T(2,128)(2,1)} reshape(bf16[32,2,4096]{2,1,0:T(2,128)(2,1)} %all-to-all-done) | data formatting | bytes 1048576
  76.6 5.0 %bitcast_reduce_fusion.1 = bf16[128,2048]{1,0:T(8,128)(2,1)} fusion(bf16[128,1,2048]{2,1,0:T(2,128)(2,1)} %reshape.295), kind=kLoop, calls=%fused_computation.362 | loop fusion | bytes 1048576 | tf_op jit(solution)/shard_map/all_to_all | solution.py:151
  98.8 45.4 %all-to-all-done.3 = bf16[2,64,4,2048]{3,2,0,1:T(4,128)(2,1)S(1)} async-done(((bf16[2,64,4,2048]{3,2,0,1:T(4,128)(2,1)}), bf16[2,64,4,2048]{3,2,0,1:T(4,128)(2,1)S(1)}, u32[]{:S(2)}, u32[]{:S(2)}) %all-to-all-start.3) | async-done | bytes 2097184 | tf_op jit(solution)/shard_map/all_to_all | solution.py:174
  156.3 41.5 %all-to-all-done.1 = bf16[2,64,4,2048]{3,2,0,1:T(4,128)(2,1)} async-done(((bf16[2,64,4,2048]{3,2,0,1:T(4,128)(2,1)}), bf16[2,64,4,2048]{3,2,0,1:T(4,128)(2,1)}, u32[]{:S(2)}, u32[]{:S(2)}) %all-to-all-start.1) | async-done | bytes 2097184 | tf_op jit(solution)/shard_map/all_to_all | solution.py:156
  210.7 4.4 %fusion.29 = f32[2,32,2048,4]{2,3,1,0:T(4,128)S(1)} fusion(f32[2,32,4,2048]{3,1,2,0:T(8,128)S(1)} %get-tuple-element.11), kind=kOutput, calls=%fused_computation.67 | convolution fusion | flops 25166048 | bytes 4194304 | tf_op jit(solution)/shard_map/eb,kcbw->kcew/dot_general | solution.py:45
  215.1 4.4 %fusion.33 = f32[2,32,2048,4]{2,3,1,0:T(4,128)S(1)} fusion(f32[2,32,4,2048]{3,1,2,0:T(8,128)S(1)} %get-tuple-element.12), kind=kOutput, calls=%fused_computation.71 | convolution fusion | flops 25166048 | bytes 4194304 | tf_op jit(solution)/shard_map/eb,kcbw->kcew/dot_general | solution.py:42
  219.6 4.7 %convolution_add_fusion.2 = f32[2,32,2048,4]{2,3,1,0:T(4,128)S(1)} fusion(f32[2,32,2048,4]{2,3,1,0:T(4,128)S(1)} %fusion.29, f32[2,32,4,2048]{3,1,2,0:T(8,128)S(1)} %get-tuple-element.12), kind=kOutput, calls=%fused_computation.10 | convolution fusion | flops 25690352 | bytes 6291456 | tf_op jit(solution)/shard_map/eb,kcbw->kcew/dot_general | solution.py:45
  224.3 4.7 %convolution_subtract_fusion.3 = f32[2,32,2048,4]{2,3,1,0:T(4,128)S(1)} fusion(f32[2,32,2048,4]{2,3,1,0:T(4,128)S(1)} %fusion.33, f32[2,32,4,2048]{3,1,2,0:T(8,128)S(1)} %get-tuple-element.11), kind=kOutput, calls=%fused_computation.12 | convolution fusion | flops 25690352 | bytes 6291456 | tf_op jit(solution)/shard_map/eb,kcbw->kcew/dot_general | solution.py:42
  229.0 4.4 %fusion.35 = f32[2,32,2048,4]{2,3,1,0:T(4,128)S(1)} fusion(f32[2,32,4,2048]{3,1,2,0:T(8,128)S(1)} %get-tuple-element.23), kind=kOutput, calls=%fused_computation.73 | convolution fusion | flops 25166048 | bytes 4194304 | tf_op jit(solution)/shard_map/eb,kcbw->kcew/dot_general | solution.py:45
  233.4 4.6 %fusion.39 = f32[2,32,2048,4]{2,3,1,0:T(4,128)S(1)} fusion(f32[2,32,4,2048]{3,1,2,0:T(8,128)S(1)} %get-tuple-element.24), kind=kOutput, calls=%fused_computation.77 | convolution fusion | flops 25166048 | bytes 4194304 | tf_op jit(solution)/shard_map/eb,kcbw->kcew/dot_general | solution.py:42
  238.0 4.9 %convolution_subtract_fusion.5 = f32[2,32,2048,4]{2,3,1,0:T(4,128)S(1)} fusion(f32[2,32,2048,4]{2,3,1,0:T(4,128)S(1)} %fusion.39, f32[2,32,4,2048]{3,1,2,0:T(8,128)S(1)} %get-tuple-element.23), kind=kOutput, calls=%fused_computation.17 | convolution fusion | flops 25690352 | bytes 6291456 | tf_op jit(solution)/shard_map/eb,kcbw->kcew/dot_general | solution.py:42
  242.9 7.3 %multiply_subtract_fusion = (f32[2,32,2048,4]{2,3,1,0:T(4,128)S(1)}, f32[2,32,2048,4]{2,3,1,0:T(4,128)S(1)}) fusion(f32[2,32,2048,4]{2,3,1,0:T(4,128)S(1)} %convolution_add_fusion.2, f32[2,32,2048,4]{2,3,1,0:T(4,128)S(1)} %convolution_subtract_fusion.5, f32[2,32,2048,4]{2,3,1,0:T(4,128)S(1)} %convolution_subtract_fusion.3, ...), kind=kOutput, calls=%fused_computation.50 | convolution fusion | flops 28836080 | bytes 14680064 | tf_op jit(solution)/shard_map/eb,kcbw->kcew/dot_general | solution.py:45
  250.2 4.0 %fusion.19 = f32[2,32,2048,4]{2,3,1,0:T(4,128)S(1)} fusion(f32[2,32,2048,4]{2,3,1,0:T(4,128)S(1)} %get-tuple-element.5), kind=kOutput, calls=%fused_computation.42 | convolution fusion | flops 25166048 | bytes 4194304 | tf_op jit(solution)/shard_map/be,kcew->kcbw/dot_general | solution.py:42
  254.3 4.0 %fusion.15 = f32[2,32,2048,4]{2,3,1,0:T(4,128)S(1)} fusion(f32[2,32,2048,4]{2,3,1,0:T(4,128)S(1)} %get-tuple-element.6), kind=kOutput, calls=%fused_computation.38 | convolution fusion | flops 25166048 | bytes 4194304 | tf_op jit(solution)/shard_map/be,kcew->kcbw/dot_general | solution.py:45
  258.3 4.2 %convolution_add_fusion.1 = f32[2,32,2048,4]{2,3,1,0:T(4,128)S(1)} fusion(f32[2,32,2048,4]{2,3,1,0:T(4,128)S(1)} %fusion.15, f32[2,32,2048,4]{2,3,1,0:T(4,128)S(1)} %get-tuple-element.5), kind=kOutput, calls=%fused_computation.8 | convolution fusion | flops 25690336 | bytes 6291456 | tf_op jit(solution)/shard_map/be,kcew->kcbw/dot_general | solution.py:45
  262.5 5.9 %subtract_bitcast_fusion = (f32[2,32,4,2048]{3,2,1,0:T(4,128)S(1)}, f32[2,32,4,2048]{3,2,1,0:T(4,128)S(1)}) fusion(f32[2,32,2048,4]{2,3,1,0:T(4,128)S(1)} %convolution_add_fusion.1, f32[32,4]{1,0:T(8,128)S(1)} %copy.169, f32[32,4]{1,0:T(8,128)S(1)} %copy.168, f32[2,32,2048,4]{2,3,1,0:T(4,128)S(1)} %fusion.19, f32[2,32,2048,4]{2,3,1,0:T(4,128)S(1)} %get-tuple-element.6), kind=kOutput, calls=%fused_computation.48 | convolution fusion | flops 28836064 | bytes 10486784 | tf_op jit(solution)/shard_map/be,kcew->kcbw/dot_general | solution.py:42
  293.8 52.2 %all_to_all.72 = bf16[2,2,128,2048]{3,1,0,2:T(2,128)(2,1)S(1)} all-to-all(bf16[2,2,128,2048]{3,1,0,2:T(2,128)(2,1)S(1)} %copy.178), channel_id=1, replica_groups=mesh['seqmaj'=4,'seqmin'=8] {'seqmaj','seqmin'}, dimensions={2} | all-to-all | bytes 4194304 | tf_op jit(solution)/shard_map/all_to_all | solution.py:189
  352.7 18.4 %all_to_all.73 = bf16[32,4,2048]{2,1,0:T(4,128)(2,1)S(1)} all-to-all(bf16[32,4,2048]{2,1,0:T(4,128)(2,1)S(1)} %convert_element_type.235), channel_id=1, replica_groups=mesh['seqmaj'=4,'seqmin'=8] {'seqmaj','seqmin'}, dimensions={0} | all-to-all | bytes 1048576 | tf_op jit(solution)/shard_map/all_to_all | solution.py:193
  371.2 5.5 %convolution_convert_fusion = bf16[128,2048]{1,0:T(8,128)(2,1)} fusion(bf16[2048,2048]{1,0:T(8,128)(2,1)} %param.23, f32[128,2048]{1,0:T(8,128)S(1)} %reshape.283, bf16[128,2048]{1,0:T(8,128)(2,1)S(1)} %fusion.10, bf16[128,2048]{1,0:T(8,128)(2,1)S(1)} %copy-done.4, f32[2048]{0:T(1024)S(1)} %copy-done.12), kind=kOutput, calls=%fused_computation.22 | convolution fusion | flops 1075576832 | bytes 11018240 | tf_op jit(solution)/shard_map/dot_general | solution.py:234
  (99 shorter events, 104.0 us)
Async XLA Ops:
  0.0 4.7 %copy-start.10 = (f32[16,2048]{1,0:T(8,128)S(1)}, f32[16,2048]{1,0:T(8,128)}, u32[]{:S(2)}) copy-start(f32[16,2048]{1,0:T(8,128)} %param.21) | copy-start | bytes 393220
  0.0 4.7 %copy-start.9 = (f32[16,2048]{1,0:T(8,128)S(1)}, f32[16,2048]{1,0:T(8,128)}, u32[]{:S(2)}) copy-start(f32[16,2048]{1,0:T(8,128)} %param.20) | copy-start | bytes 393220
  1.5 23.9 %collective-permute-start = (bf16[127,2048]{1,0:T(8,128)(2,1)S(1)}, bf16[127,2048]{1,0:T(8,128)(2,1)}, u32[]{:S(2)}, u32[]{:S(2)}) collective-permute-start(bf16[127,2048]{1,0:T(8,128)(2,1)S(1)} %slice.34), channel_id=1, source_target_pairs={{0,1},{1,2},{2,3},{3,4},{4,5},{5,6},{6,7},{7,8},{8,9},{9,10},{10,1... | collective-permute-start | bytes 1560584 | tf_op jit(solution)/shard_map/ppermute | solution.py:18
  8.4 11.9 %copy-start.7 = (bf16[128,2048]{1,0:T(8,128)(2,1)S(1)}, bf16[128,2048]{1,0:T(8,128)(2,1)}, u32[]{:S(2)}) copy-start(bf16[128,2048]{1,0:T(8,128)(2,1)} %param.15) | copy-start | bytes 1572868
  13.7 35.4 %all-to-all-start.2 = ((bf16[32,2,4096]{2,1,0:T(2,128)(2,1)}), bf16[32,2,4096]{2,1,0:T(2,128)(2,1)S(1)}, u32[]{:S(2)}, u32[]{:S(2)}) async-start(bf16[32,2,4096]{2,1,0:T(2,128)(2,1)} %reshape.296), calls=%async_computation.2 | async-start | bytes 1048576 | tf_op jit(solution)/shard_map/all_to_all | solution.py:166
  25.4 1.4 copy-start.8
  25.4 16.3 %slice-start = ((s8[8388608]{0:T(1024)(128)(4,1)}), s8[4194304]{0:T(1024)(128)(4,1)S(1)}, s32[]{:S(2)}) async-start(s8[8388608]{0:T(1024)(128)(4,1)} %bitcast.222), calls=%async_computation.6 | async-start | bytes 8388608
  26.8 14.9 %slice-start.1 = ((s8[8388608]{0:T(1024)(128)(4,1)}), s8[4194304]{0:T(1024)(128)(4,1)S(1)}, s32[]{:S(2)}) async-start(s8[8388608]{0:T(1024)(128)(4,1)} %bitcast.222), calls=%async_computation.7 | async-start | bytes 8388608
  26.8 14.9 %copy-start.5 = (bf16[128,2048]{1,0:T(8,128)(2,1)S(1)}, bf16[128,2048]{1,0:T(8,128)(2,1)}, u32[]{:S(2)}) copy-start(bf16[128,2048]{1,0:T(8,128)(2,1)} %param.12) | copy-start | bytes 1572868
  26.8 14.9 %copy-start.6 = (bf16[128,2048]{1,0:T(8,128)(2,1)S(1)}, bf16[128,2048]{1,0:T(8,128)(2,1)}, u32[]{:S(2)}) copy-start(bf16[128,2048]{1,0:T(8,128)(2,1)} %param.19) | copy-start | bytes 1572868
  26.8 14.9 %copy-start.11 = (f32[2048]{0:T(1024)S(1)}, f32[2048]{0:T(1024)}, u32[]{:S(2)}) copy-start(f32[2048]{0:T(1024)} %param.16) | copy-start | bytes 24580
  49.1 22.6 %all-to-all-start = ((bf16[32,2,4096]{2,1,0:T(2,128)(2,1)}), bf16[32,2,4096]{2,1,0:T(2,128)(2,1)}, u32[]{:S(2)}, u32[]{:S(2)}) async-start(bf16[32,2,4096]{2,1,0:T(2,128)(2,1)} %reshape.294), calls=%async_computation | async-start | bytes 1048576 | tf_op jit(solution)/shard_map/all_to_all | solution.py:151
  83.1 1.6 copy-start
  91.3 52.8 %all-to-all-start.3 = ((bf16[2,64,4,2048]{3,2,0,1:T(4,128)(2,1)}), bf16[2,64,4,2048]{3,2,0,1:T(4,128)(2,1)S(1)}, u32[]{:S(2)}, u32[]{:S(2)}) async-start(bf16[2,64,4,2048]{3,2,0,1:T(4,128)(2,1)} %copy.159), calls=%async_computation.3 | async-start | bytes 4194304 | tf_op jit(solution)/shard_map/all_to_all | solution.py:174
  144.2 3.8 copy-start.2
  144.2 53.7 %all-to-all-start.1 = ((bf16[2,64,4,2048]{3,2,0,1:T(4,128)(2,1)}), bf16[2,64,4,2048]{3,2,0,1:T(4,128)(2,1)}, u32[]{:S(2)}, u32[]{:S(2)}) async-start(bf16[2,64,4,2048]{3,2,0,1:T(4,128)(2,1)} %copy.151), calls=%async_computation.1 | async-start | bytes 4194304 | tf_op jit(solution)/shard_map/all_to_all | solution.py:156
  201.7 1.6 copy-start.1
  205.9 1.6 copy-start.3
  352.3 18.9 %copy-start.4 = (bf16[128,2048]{1,0:T(8,128)(2,1)S(1)}, bf16[128,2048]{1,0:T(8,128)(2,1)}, u32[]{:S(2)}) copy-start(bf16[128,2048]{1,0:T(8,128)(2,1)} %param.18) | copy-start | bytes 1572868
  352.3 18.9 %copy-start.12 = (f32[2048]{0:T(1024)S(1)}, f32[2048]{0:T(1024)}, u32[]{:S(2)}) copy-start(f32[2048]{0:T(1024)} %param.22) | copy-start | bytes 24580
where the time goes:
time: 384 us; the launch traced here: 377 us
  matrix products  117 us (30%)
  waiting for transfers between devices  95.6 us (25%)
  blocking collectives  70.6 us (18%)
  local copies, waits for them, and re-layouts  49.3 us (13%)
  starting transfers between devices  22.5 us (6%)
  other arithmetic  21 us (5%)
    all_to_all x1, blocking collectives, long_convolution(): lax.all_to_all(shortened(turned), ('seqmaj', 'seqmin'), split_axis=2, con...  52.2 us
    all_to_all x1, waiting for transfers between devices, long_convolution(): lax.all_to_all(shortened(filter_spread), ('seqmaj', 'seqmin'), split_axis...  45.4 us
    all_to_all x1, waiting for transfers between devices, long_convolution(): lax.all_to_all(shortened(spread), ('seqmaj', 'seqmin'), split_axis=1, con...  41.5 us
    dot_general x6, matrix products, complex_product(): jnp.einsum(pattern, table_im, data_re, precision=highest)  24.3 us
    dot_general x6, matrix products, complex_product(): jnp.einsum(pattern, table_im, data_im, precision=highest)  21.5 us
    dot_general x6, matrix products, complex_product(): jnp.einsum(pattern, table_re, data_re, precision=highest)  20 us
    dot_general x6, matrix products, complex_product(): jnp.einsum(pattern, table_re, data_im, precision=highest)  19.8 us
    all_to_all x1, blocking collectives, long_convolution(): lax.all_to_all(shortened(values), ('seqmaj', 'seqmin'), split_axis=0, con...  18.4 us
  transfers between devices with their start and end apart: 5, of which 3 were waited for; matrix products, arithmetic and copies ran while one was open for 15% of the time, Pallas kernels for 0%

commit v1 on v0

v1 whole, which is shorter than its diff:
```python
import jax
import jax.numpy as jnp
import numpy as np
from jax import lax
from jax.sharding import PartitionSpec as P

axes = ("seqmaj", "seqmin")


def dft_tables(rows):
    size = 2 * rows
    theta = 2.0 * np.pi * (np.arange(rows) + 0.5) / size
    angle = theta[:, None] * np.arange(size)[None, :]
    forward = np.concatenate([np.cos(angle), np.sin(angle)], axis=0)
    inverse = forward.T / rows
    return forward.astype(np.float32), inverse.astype(np.float32)


def mm(a, b):
    return jnp.dot(a.astype(jnp.bfloat16), b.astype(jnp.bfloat16), preferred_element_type=jnp.float32)


def spectral_product(x, h):
    n = x.shape[0] // 2
    xc, xs, hc, hs = x[:n], x[n:], h[:n], h[n:]
    return jnp.concatenate([xc * hc - xs * hs, xc * hs + xs * hc], axis=0)


def local(q1, k1, v1, taps, skip1, w1, q2, k2, residue, rate, skip2, w2):
    f32, bf16 = jnp.float32, jnp.bfloat16
    rows, channels = q1.shape
    modes = rate.shape[0]
    minor = lax.axis_size("seqmin")
    n = lax.axis_size("seqmaj") * minor
    fwd, inv = dft_tables(rows)
    g1 = (k1.astype(f32) * v1.astype(f32)).astype(bf16)
    border = lax.ppermute(g1, axes, [(i, i + 1) for i in range(n - 1)])
    window = jnp.concatenate([border, g1], axis=0)
    spec = spectral_product(mm(fwd, window), mm(fwd[:, :rows], taps))
    short = mm(inv[rows:], spec)
    act1 = (q1.astype(f32) * (short + skip1[None, :] * g1.astype(f32))).astype(bf16)
    v2 = jnp.dot(act1, w1, preferred_element_type=f32).astype(bf16)
    g2 = (k2.astype(f32) * v2.astype(f32)).astype(bf16)
    g2f = g2.astype(f32)
    t = jnp.arange(rows, dtype=f32)
    weight = residue * jnp.sqrt(rate)
    powers = jnp.exp(-rate[None] * t[:, None, None])
    head = jnp.sum(weight[None] * powers, axis=1)
    spec2 = spectral_product(mm(fwd[:, :rows], g2), mm(fwd[:, :rows], head))
    near = mm(inv[:rows], spec2)
    ends = jnp.sum(jnp.exp(-rate[None] * (rows - 1.0 - t)[:, None, None]) * g2f[:, None, :], axis=0)
    flat = modes * channels // n
    got = lax.all_to_all(ends.reshape(n, flat).astype(bf16), axes, 0, 0, tiled=True).astype(f32)
    device = lax.axis_index("seqmaj") * minor + lax.axis_index("seqmin")
    own_rate = lax.dynamic_index_in_dim(rate.reshape(n, flat), device, 0, keepdims=False)
    d = jnp.arange(n, dtype=f32)
    lag = d[:, None] - 1.0 - d[None, :]
    decay = jnp.where(lag[:, :, None] >= 0, jnp.exp(-own_rate * (rows * jnp.maximum(lag, 0.0))[:, :, None]), 0.0)
    carry = jnp.sum(decay * got[None], axis=1)
    state = lax.all_to_all(carry.astype(bf16), axes, 0, 0, tiled=True).astype(f32).reshape(modes, channels)
    far = jnp.sum((weight * state)[None] * jnp.exp(-rate[None] * (t + 1.0)[:, None, None]), axis=1)
    act2 = (q2.astype(f32) * (near + far + skip2[None, :] * g2f)).astype(bf16)
    return jnp.dot(act2, w2, preferred_element_type=f32).astype(bf16)


def solution(mesh):
    s, r = P(axes, None), P()
    specs = (s, s, s, r, r, r, s, s, r, r, r, r)
    return jax.shard_map(local, mesh=mesh, in_specs=specs, out_specs=s, check_vma=False)
```

time: 384 us -> 81 us (0.21); the launches traced: 377 us -> 80.4 us
  matrix products: 117 us -> 29.4 us
  waiting for transfers between devices: 95.6 us -> 8.46 us
  blocking collectives: 70.6 us -> 0 us
  local copies, waits for them, and re-layouts: 49.3 us -> 5.98 us
  starting transfers between devices: 22.5 us -> 12.4 us
    all_to_all x4 -> x2, waiting for transfers between devices: 95.6 us -> 8.46 us  [the longest x1 4.3 us: local(): lax.all_to_all(carry.astype(bf16), axes, 0, 0, tiled=True).astype(f32)]
    dot_general x32 -> x9, matrix products: 102 us -> 29.4 us  [the longest x7 14.6 us: mm(): jnp.dot(a.astype(jnp.bfloat16), b.astype(jnp.bfloat16), preferred_element...]
    all_to_all x2 -> x0, blocking collectives: 70.6 us -> none  [the longest x1 52.2 us: long_convolution(): lax.all_to_all(shortened(turned), ('seqmaj', 'seqmin'), split_axis=2, con...]
    all_to_all x5 -> x0, local copies, waits for them, and re-layouts: 16.2 us -> none  [the longest x1 5.04 us: long_convolution(): lax.all_to_all(signal[None], ('seqmaj', 'seqmin'), split_axis=1, concat_a...]
    reduce_sum x1 -> x3, other arithmetic: 2.78 us -> 18.6 us  [the longest x1 9.9 us: local(): head = jnp.sum(weight[None] * powers, axis=1)]
    conv_general_dilated x1 -> x0, matrix products: 14.9 us -> none  [tap_convolution(): lax.conv_general_dilated(window[None], flipped, (1,), 'VALID', dimension_...]
    all_to_all x4 -> x2, starting transfers between devices: 19.4 us -> 9.85 us  [the longest x1 7.1 us: local(): lax.all_to_all(ends.reshape(n, flat).astype(bf16), axes, 0, 0, tiled=True)]
    another operation x3 -> x0, local copies, waits for them, and re-layouts: 8.42 us -> none  [the longest x2 5.88 us: forward_outer(): jnp.stack([part_re * twist_re - part_im * twist_im, part_re * twist_im +...]
  transfers between devices with their start and end apart: 5 -> 3, of which waited for: 3 -> 2; matrix products, arithmetic and copies ran while one was open for 15% -> 18% of each run, Pallas kernels for 0% -> 0%
where the time goes in v1:
time: 81 us; the launch traced here: 80.4 us
  matrix products  29.4 us (36%)
  other arithmetic  24 us (30%)
  starting transfers between devices  12.4 us (15%)
  waiting for transfers between devices  8.46 us (10%)
  local copies, waits for them, and re-layouts  5.98 us (7%)
    dot_general x7, matrix products, mm(): jnp.dot(a.astype(jnp.bfloat16), b.astype(jnp.bfloat16), preferred_element...  14.6 us
    reduce_sum x1, other arithmetic, local(): head = jnp.sum(weight[None] * powers, axis=1)  9.9 us
    dot_general x1, matrix products, local(): v2 = jnp.dot(act1, w1, preferred_element_type=f32).astype(bf16)  7.41 us
    dot_general x1, matrix products, local(): return jnp.dot(act2, w2, preferred_element_type=f32).astype(bf16)  7.36 us
    reduce_sum x1, other arithmetic, local(): jnp.sum((weight * state)[None] * jnp.exp(-rate[None] * (t + 1.0)[:, None,...  7.16 us
    all_to_all x1, starting transfers between devices, local(): lax.all_to_all(ends.reshape(n, flat).astype(bf16), axes, 0, 0, tiled=True)  7.1 us
    unnamed x38, local copies, waits for them, and re-layouts  5.24 us
    all_to_all x1, waiting for transfers between devices, local(): lax.all_to_all(carry.astype(bf16), axes, 0, 0, tiled=True).astype(f32)  4.3 us
  transfers between devices with their start and end apart: 3, of which 2 were waited for; matrix products, arithmetic and copies ran while one was open for 18% of the time, Pallas kernels for 0%

profile of v1, /device:TPU:0, one launch (start us, length us, event | category | flops | bytes accessed | tf_op | source)
XLA Modules:
  0.0 80.4 jit_solution(1297378619137597458)
XLA Ops:
  0.0 1.4 %copy.33 = bf16[128,2048]{0,1:T(8,128)(2,1)S(1)} copy(bf16[128,2048]{1,0:T(8,128)(2,1)} %param.19) | data formatting | bytes 1048576 | tf_op args[1]
  1.4 1.3 %copy.34 = bf16[128,2048]{0,1:T(8,128)(2,1)S(1)} copy(bf16[128,2048]{1,0:T(8,128)(2,1)} %param.20) | data formatting | bytes 1048576 | tf_op args[2]
  2.9 2.5 %collective-permute-start = (bf16[128,2048]{0,1:T(8,128)(2,1)S(1)}, bf16[128,2048]{0,1:T(8,128)(2,1)S(1)}, u32[]{:S(2)}, u32[]{:S(2)}) collective-permute-start(bf16[128,2048]{0,1:T(8,128)(2,1)S(1)} %multiply_convert_fusion), channel_id=1, source_target_pairs={{0,1},{1,2},{2,3},{3,4},{4,5},{5,6},{6,7},{7,8},{8,9},{9,10},{10,1... | collective-permute-start | bytes 1572872 | tf_op jit(solution)/shard_map/ppermute | solution.py:37
  6.7 2.6 %fusion.28 = f32[2048,256]{1,0:T(8,128)} fusion(bf16[128,2048]{0,1:T(8,128)(2,1)S(1)} %multiply_convert_fusion, bf16[256,128]{1,0:T(8,128)(2,1)} %constant.42), kind=kOutput, calls=%fused_computation.52 | convolution fusion | flops 134217728 | bytes 2686976 | tf_op jit(solution)/shard_map/dot_general | solution.py:20
  9.3 1.0 %copy.32 = bf16[128,2048]{0,1:T(8,128)(2,1)} copy(bf16[128,2048]{1,0:T(8,128)(2,1)S(1)} %copy-done.4) | data formatting | bytes 1048576 | tf_op args[0]
  10.4 1.8 %fusion.29 = f32[256,2048]{0,1:T(8,128)} fusion(bf16[256,128]{1,0:T(8,128)(2,1)S(1)} %copy-done.3, bf16[128,2048]{1,0:T(8,128)(2,1)S(1)} %copy-done), kind=kOutput, calls=%fused_computation.53 | convolution fusion | flops 134217728 | bytes 2686976 | tf_op jit(solution)/shard_map/dot_general | solution.py:20
  13.4 0.7 fusion.26
  14.1 2.0 %fusion = f32[256,2048]{0,1:T(8,128)S(1)} fusion(f32[2048,256]{1,0:T(8,128)} %fusion.28, bf16[128,2048]{0,1:T(8,128)(2,1)S(1)} %collective-permute-done, bf16[256,128]{1,0:T(8,128)(2,1)S(1)} %copy-done.3), kind=kOutput, calls=%fused_computation.5 | convolution fusion | flops 134742016 | bytes 4784128 | tf_op jit(solution)/shard_map/dot_general | solution.py:20
  16.1 2.1 %fusion.18 = f32[2048,128]{1,0:T(8,128)} fusion(bf16[128,128]{1,0:T(8,128)(2,1)} %constant.43, f32[256,2048]{0,1:T(8,128)S(1)} %copy-done.1, f32[256,2048]{0,1:T(8,128)S(1)} %fusion), kind=kOutput, calls=%fused_computation.32 | convolution fusion | flops 68157440 | bytes 5275648 | tf_op jit(solution)/shard_map/dot_general | solution.py:20
  18.2 7.4 %fusion.27 = (f32[128,2048]{1,0:T(8,128)}, bf16[128,2048]{1,0:T(8,128)(2,1)S(1)}) fusion(bf16[2048,2048]{1,0:T(8,128)(2,1)} %param.23, f32[2048,128]{1,0:T(8,128)} %fusion.18, bf16[128,128]{1,0:T(8,128)(2,1)S(1)} %copy-done.10, bf16[128,2048]{0,1:T(8,128)(2,1)} %copy-done.2, bf16[128,2048]{0,1:T(8,128)(2,1)} %copy.32, f32[256,2048]{0,1:T(8,128)} %fusion.29, ...), kind=kOutput, calls=%fused_computation.51 | convolution fusion | flops 1145307136 | bytes 16818176 | tf_op jit(solution)/shard_map/dot_general | solution.py:42
  25.6 9.9 %multiply_reduce_fusion.2 = (bf16[128,2048]{1,0:T(8,128)(2,1)}, bf16[16,2048]{1,0:T(8,128)(2,1)S(1)}) fusion(f32[16,2048]{1,0:T(8,128)S(1)} %copy-done.7, f32[16,2048]{1,0:T(8,128)S(1)} %get-tuple-element.8, f32[128,2048]{1,0:T(8,128)} %get-tuple-element.9, f32[128]{0:T(128)} %iota_subtract_fusion.1), kind=kLoop, calls=%fused_computation.2 | loop fusion | flops 24870912 | bytes 1901056 | tf_op jit(solution)/shard_map/reduce_sum | solution.py:48
  36.2 1.0 %reduce.2 = bf16[32,1024]{1,0:T(8,128)(2,1)S(1)} reduce(bf16[32,1,1024]{2,1,0:T(2,128)(2,1)S(1)} %convert_element_type.115, bf16[]{:T(256)} %broadcast.63), dimensions={1}, to_apply=%convert_element_type.115.reduce_sub_computation | reduce | bytes 131074 | tf_op jit(solution)/shard_map/convert_element_type | solution.py:53
  37.2 0.7 reshape.110
  37.9 7.1 %all-to-all-start = ((bf16[32,2,512]{2,1,0:T(2,128)(2,1)}), bf16[32,2,512]{2,1,0:T(2,128)(2,1)S(1)}, u32[]{:S(2)}, u32[]{:S(2)}) async-start(bf16[32,2,512]{2,1,0:T(2,128)(2,1)} %reshape.110), calls=%async_computation | async-start | bytes 131072 | tf_op jit(solution)/shard_map/all_to_all | solution.py:53
  45.0 1.5 %fusion.31 = f32[256,2048]{1,0:T(8,128)S(1)} fusion(bf16[256,128]{1,0:T(8,128)(2,1)S(1)} %copy-done.3, bf16[128,2048]{1,0:T(8,128)(2,1)} %get-tuple-element.5), kind=kOutput, calls=%fused_computation.55 | convolution fusion | flops 134217728 | bytes 2686976 | tf_op jit(solution)/shard_map/dot_general | solution.py:20
  46.5 1.8 %fusion.30 = f32[256,2048]{1,0:T(8,128)} fusion(bf16[256,128]{1,0:T(8,128)(2,1)S(1)} %copy-done.3, bf16[128,2048]{1,0:T(8,128)(2,1)S(1)} %get-tuple-element.10), kind=kOutput, calls=%fused_computation.54 | convolution fusion | flops 134217728 | bytes 2686976 | tf_op jit(solution)/shard_map/dot_general | solution.py:20
  48.2 4.2 %all-to-all-done = bf16[32,2,512]{2,1,0:T(2,128)(2,1)S(1)} async-done(((bf16[32,2,512]{2,1,0:T(2,128)(2,1)}), bf16[32,2,512]{2,1,0:T(2,128)(2,1)S(1)}, u32[]{:S(2)}, u32[]{:S(2)}) %all-to-all-start) | async-done | bytes 65568 | tf_op jit(solution)/shard_map/all_to_all | solution.py:53
  52.5 1.5 %multiply_reduce_fusion.3 = bf16[32,1024]{1,0:T(8,128)(2,1)S(1)} fusion(f32[32,1024]{1,0:T(8,128)S(1)} %bitcast.49, f32[32,32]{1,0:T(8,128)S(1)} %maximum_multiply_fusion, f32[1024]{0:T(1024)S(1)} %bitcast.51, pred[32,32]{1,0:T(8,128)(4,1)S(1)} %copy-done.13), kind=kLoop, calls=%fused_computation.3 | loop fusion | flops 4161536 | bytes 205824 | tf_op jit(solution)/shard_map/reduce_sum | solution.py:59
  54.0 0.7 reduce.3
  55.4 2.8 %all-to-all-start.1 = ((bf16[32,2,512]{2,1,0:T(2,128)(2,1)}), bf16[32,2,512]{2,1,0:T(2,128)(2,1)S(1)}, u32[]{:S(2)}, u32[]{:S(2)}) async-start(bf16[32,2,512]{2,1,0:T(2,128)(2,1)} %reshape.112), calls=%async_computation.1 | async-start | bytes 131072 | tf_op jit(solution)/shard_map/all_to_all | solution.py:60
  58.2 2.9 %fusion.19 = f32[2048,128]{0,1:T(8,128)} fusion(bf16[128,128]{1,0:T(8,128)(2,1)S(1)} %copy-done.9, f32[256,2048]{1,0:T(8,128)S(1)} %fusion.31, f32[256,2048]{1,0:T(8,128)} %fusion.30), kind=kOutput, calls=%fused_computation.33 | convolution fusion | flops 68157440 | bytes 5275648 | tf_op jit(solution)/shard_map/dot_general | solution.py:20
  61.1 4.3 %all-to-all-done.1 = bf16[32,2,512]{2,1,0:T(2,128)(2,1)S(1)} async-done(((bf16[32,2,512]{2,1,0:T(2,128)(2,1)}), bf16[32,2,512]{2,1,0:T(2,128)(2,1)S(1)}, u32[]{:S(2)}, u32[]{:S(2)}) %all-to-all-start.1) | async-done | bytes 65568 | tf_op jit(solution)/shard_map/all_to_all | solution.py:60
  65.9 7.2 %multiply_reduce_fusion = f32[128,2048]{1,0:T(8,128)} fusion(f32[128]{0:T(128)} %iota_add_fusion, f32[16,2048]{1,0:T(8,128)S(1)} %mul.182, f32[16,2048]{1,0:T(8,128)} %get-tuple-element.7), kind=kLoop, calls=%fused_computation | loop fusion | flops 12320768 | bytes 1311232 | tf_op jit(solution)/shard_map/reduce_sum | solution.py:61
  73.0 7.4 %convolution_convert_fusion = bf16[128,2048]{1,0:T(8,128)(2,1)} fusion(bf16[2048,2048]{1,0:T(8,128)(2,1)} %param.29, f32[128,2048]{1,0:T(8,128)} %multiply_reduce_fusion, f32[2048,128]{0,1:T(8,128)} %fusion.19, bf16[128,128]{1,0:T(8,128)(2,1)S(1)} %copy-done.8, bf16[128,2048]{1,0:T(8,128)(2,1)} %param.24, f32[256,2048]{1,0:T(8,128)S(1)} %fusion.31, ...), kind=kOutput, calls=%fused_computation.16 | convolution fusion | flops 1144258560 | bytes 16293888 | tf_op jit(solution)/shard_map/dot_general | solution.py:63
  (48 shorter events, 4.6 us)
Async XLA Ops:
  0.0 10.3 %copy-start = (bf16[128,2048]{1,0:T(8,128)(2,1)S(1)}, bf16[128,2048]{1,0:T(8,128)(2,1)}, u32[]{:S(2)}) copy-start(bf16[128,2048]{1,0:T(8,128)(2,1)} %param.21) | copy-start | bytes 1572868
  0.0 10.4 %copy-start.3 = (bf16[256,128]{1,0:T(8,128)(2,1)S(1)}, bf16[256,128]{1,0:T(8,128)(2,1)}, u32[]{:S(2)}) copy-start(bf16[256,128]{1,0:T(8,128)(2,1)} %constant.38.clone) | copy-start | bytes 196612
  0.0 9.3 %copy-start.4 = (bf16[128,2048]{1,0:T(8,128)(2,1)S(1)}, bf16[128,2048]{1,0:T(8,128)(2,1)}, u32[]{:S(2)}) copy-start(bf16[128,2048]{1,0:T(8,128)(2,1)} %param.18) | copy-start | bytes 1572868
  0.0 10.3 %copy-start.5 = (f32[16,2048]{1,0:T(8,128)S(1)}, f32[16,2048]{1,0:T(8,128)}, u32[]{:S(2)}) copy-start(f32[16,2048]{1,0:T(8,128)} %param.27) | copy-start | bytes 393220
  2.9 11.2 %copy-start.2 = (bf16[128,2048]{0,1:T(8,128)(2,1)}, bf16[128,2048]{0,1:T(8,128)(2,1)S(1)}, u32[]{:S(2)}) copy-start(bf16[128,2048]{0,1:T(8,128)(2,1)S(1)} %multiply_convert_fusion) | copy-start | bytes 1572868
  2.9 10.5 %copy-start.6 = (f32[16,2048]{1,0:T(8,128)S(1)}, f32[16,2048]{1,0:T(8,128)}, u32[]{:S(2)}) copy-start(f32[16,2048]{1,0:T(8,128)} %param.26) | copy-start | bytes 393220
  2.9 11.2 %collective-permute-start = (bf16[128,2048]{0,1:T(8,128)(2,1)S(1)}, bf16[128,2048]{0,1:T(8,128)(2,1)S(1)}, u32[]{:S(2)}, u32[]{:S(2)}) collective-permute-start(bf16[128,2048]{0,1:T(8,128)(2,1)S(1)} %multiply_convert_fusion), channel_id=1, source_target_pairs={{0,1},{1,2},{2,3},{3,4},{4,5},{5,6},{6,7},{7,8},{8,9},{9,10},{10,1... | collective-permute-start | bytes 1572872 | tf_op jit(solution)/shard_map/ppermute | solution.py:37
  12.2 3.9 %copy-start.1 = (f32[256,2048]{0,1:T(8,128)S(1)}, f32[256,2048]{0,1:T(8,128)}, u32[]{:S(2)}) copy-start(f32[256,2048]{0,1:T(8,128)} %fusion.29) | copy-start | bytes 6291460
  13.4 4.8 %copy-start.10 = (bf16[128,128]{1,0:T(8,128)(2,1)S(1)}, bf16[128,128]{1,0:T(8,128)(2,1)}, u32[]{:S(2)}) copy-start(bf16[128,128]{1,0:T(8,128)(2,1)} %constant.44) | copy-start | bytes 98308
  13.4 4.8 %copy-start.11 = (f32[2048]{0:T(1024)S(1)}, f32[2048]{0:T(1024)}, u32[]{:S(2)}) copy-start(f32[2048]{0:T(1024)} %param.22) | copy-start | bytes 24580
  18.2 7.4 %copy-start.7 = (f32[16,2048]{1,0:T(8,128)S(1)}, f32[16,2048]{1,0:T(8,128)}, u32[]{:S(2)}) copy-start(f32[16,2048]{1,0:T(8,128)} %get-tuple-element.7) | copy-start | bytes 393220
  35.5 17.0 %copy-start.13 = (pred[32,32]{1,0:T(8,128)(4,1)S(1)}, pred[32,32]{1,0:T(8,128)(4,1)}, u32[]{:S(2)}) copy-start(pred[32,32]{1,0:T(8,128)(4,1)} %fusion.25) | copy-start | bytes 3076
  35.5 17.0 %copy-start.14 = (f32[1,1024]{1,0:T(1,128)S(1)}, f32[1,1024]{1,0:T(1,128)}, u32[]{:S(2)}) copy-start(f32[1,1024]{1,0:T(1,128)} %dynamic-slice_negate_fusion) | copy-start | bytes 12292
  37.9 20.2 %copy-start.9 = (bf16[128,128]{1,0:T(8,128)(2,1)S(1)}, bf16[128,128]{1,0:T(8,128)(2,1)}, u32[]{:S(2)}) copy-start(bf16[128,128]{1,0:T(8,128)(2,1)} %constant.45) | copy-start | bytes 98308
  37.9 14.5 %all-to-all-start = ((bf16[32,2,512]{2,1,0:T(2,128)(2,1)}), bf16[32,2,512]{2,1,0:T(2,128)(2,1)S(1)}, u32[]{:S(2)}, u32[]{:S(2)}) async-start(bf16[32,2,512]{2,1,0:T(2,128)(2,1)} %reshape.110), calls=%async_computation | async-start | bytes 131072 | tf_op jit(solution)/shard_map/all_to_all | solution.py:53
  55.4 10.0 %all-to-all-start.1 = ((bf16[32,2,512]{2,1,0:T(2,128)(2,1)}), bf16[32,2,512]{2,1,0:T(2,128)(2,1)S(1)}, u32[]{:S(2)}, u32[]{:S(2)}) async-start(bf16[32,2,512]{2,1,0:T(2,128)(2,1)} %reshape.112), calls=%async_computation.1 | async-start | bytes 131072 | tf_op jit(solution)/shard_map/all_to_all | solution.py:60
  65.8 7.2 %copy-start.8 = (bf16[128,128]{1,0:T(8,128)(2,1)S(1)}, bf16[128,128]{1,0:T(8,128)(2,1)}, u32[]{:S(2)}) copy-start(bf16[128,128]{1,0:T(8,128)(2,1)} %constant.46) | copy-start | bytes 98308
  65.8 7.2 %copy-start.12 = (f32[2048]{0:T(1024)S(1)}, f32[2048]{0:T(1024)}, u32[]{:S(2)}) copy-start(f32[2048]{0:T(1024)} %param.28) | copy-start | bytes 24580

commit v2 on v1

v2 whole, which is shorter than its diff:
```python
import functools

import jax
import jax.numpy as jnp
import numpy as np
from jax import lax
from jax.experimental import pallas as pl
from jax.experimental.pallas import tpu as pltpu
from jax.sharding import PartitionSpec as P

axes = ("seqmaj", "seqmin")
MESH = pl.DeviceIdType.MESH
f32, bf16 = jnp.float32, jnp.bfloat16
WIDE = 256
LANES = 128
SUB = 8


def dft_tables(rows):
    size = 2 * rows
    theta = 2.0 * np.pi * (np.arange(rows) + 0.5) / size
    angle = theta[:, None] * np.arange(size)[None, :]
    forward = np.concatenate([np.cos(angle), np.sin(angle)], axis=0)
    inverse = forward.T / rows
    return jnp.asarray(forward, bf16), jnp.asarray(inverse, bf16)


def mm(a, b):
    return jnp.dot(a, b, preferred_element_type=f32)


def spectral_product(x, h):
    half = x.shape[0] // 2
    xc, xs, hc, hs = x[:half], x[half:], h[:half], h[half:]
    return jnp.concatenate([xc * hc - xs * hs, xc * hs + xs * hc], axis=0).astype(bf16)


def kernel(
    n, minor, q1h, k1h, v1h, tapsh, skip1h, w1h, q2h, k2h, resh, rateh, skip2h, w2h, fwdh, invh, out,
    q1, k1, v1, taps, skip1, w1, q2, k2, res, rate, skip2, w2, fwd, inv,
    win, h1, h2, a8, p7, p1, head, acc, y, g2, ends, got, sout, sin, tiled_rate,
    in_sem, w1_sem, w2_sem, bsend, brecv, esend, erecv, ssend, srecv,
):
    rows, channels = q1.shape
    modes = rate.shape[0]
    chunks = channels // WIDE
    blocks = channels // LANES
    per_tile = n * SUB * LANES // (modes * channels)
    part = SUB // per_tile
    me = lax.axis_index("seqmaj") * minor + lax.axis_index("seqmin")

    def place(d):
        return (lax.div(d, minor), lax.rem(d, minor))

    def load(i, src, dst):
        return pltpu.make_async_copy(src, dst, in_sem.at[i])

    loads = {}
    for i, (name, src, dst) in enumerate([
        ("k1", k1h, k1), ("v1", v1h, v1), ("fwd", fwdh, fwd), ("taps", tapsh, taps), ("rate", rateh, rate),
        ("res", resh, res), ("inv", invh, inv), ("q1", q1h, q1), ("skip1", skip1h, skip1), ("k2", k2h, k2),
        ("skip2", skip2h, skip2), ("q2", q2h, q2),
    ]):
        loads[name] = load(i, src, dst)
        loads[name].start()

    def weight_load(src, dst, sem, c):
        span = pl.ds(pl.multiple_of(c * WIDE, WIDE), WIDE)
        return pltpu.make_async_copy(src.at[span, :], dst.at[span, :], sem.at[c])

    @pl.loop(0, chunks)
    def _(c):
        weight_load(w1h, w1, w1_sem, c).start()

    barrier = pltpu.get_barrier_semaphore()

    @pl.loop(1, n)
    def _(p):
        pl.semaphore_signal(barrier, inc=1, device_id=place(lax.rem(me + p, n)), device_id_type=MESH)

    @pl.loop(0, chunks)
    def _(c):
        weight_load(w2h, w2, w2_sem, c).start()

    def wide(c):
        return pl.ds(pl.multiple_of(c * WIDE, WIDE), WIDE)

    loads["k1"].wait()
    loads["v1"].wait()

    @pl.loop(0, chunks)
    def _(c):
        cols = wide(c)
        win[c, rows:, :] = (k1[:, cols].astype(f32) * v1[:, cols].astype(f32)).astype(bf16)

    pl.semaphore_wait(barrier, n - 1)

    def border(c):
        return pltpu.make_async_remote_copy(
            src_ref=win.at[c, pl.ds(rows, rows), :], dst_ref=win.at[c, pl.ds(0, rows), :],
            send_sem=bsend.at[c], recv_sem=brecv.at[c],
            device_id=place(lax.rem(me + 1, n)), device_id_type=MESH,
        )

    @pl.when(me < n - 1)
    def _():
        @pl.loop(0, chunks)
        def _(c):
            border(c).start()

    @pl.when(me == 0)
    def _():
        @pl.loop(0, chunks)
        def _(c):
            win[c, :rows, :] = jnp.zeros((rows, WIDE), bf16)

    loads["fwd"].wait()
    loads["taps"].wait()
    loads["rate"].wait()
    loads["res"].wait()
    step = lax.broadcasted_iota(jnp.int32, (modes, SUB, LANES), 1).astype(f32)

    def spread(ref, b):
        cols = pl.ds(pl.multiple_of(b * LANES, LANES), LANES)
        return jnp.stack([jnp.broadcast_to(ref[r : r + 1, cols], (SUB, LANES)) for r in range(modes)])

    @pl.loop(0, chunks)
    def _(c):
        h1[c] = mm(fwd[:, :rows], taps[:, wide(c)])
        for j in range(WIDE // LANES):
            b = c * (WIDE // LANES) + j
            lam = spread(rate, b)
            weight = spread(res, b) * jnp.sqrt(lam)
            decay = jnp.exp(-SUB * lam)
            a8[b] = decay
            lanes = rate[:, pl.ds(pl.multiple_of(b * LANES, LANES), LANES)]
            for hi in range(modes // SUB):
                for s in range(per_tile):
                    start = hi * SUB + s * part
                    tiled_rate[(hi * blocks + b) * per_tile + s] = lanes[start : start + part]
            p7[b] = jnp.exp(-lam * (SUB - 1.0 - step))
            p1[b] = weight * jnp.exp(-lam * (step + 1.0))
            u = weight * jnp.exp(-lam * step)
            for m in range(rows // SUB):
                head[m * SUB : (m + 1) * SUB, j * LANES : (j + 1) * LANES] = jnp.sum(u, axis=0)
                u = u * decay
        h2[c] = mm(fwd[:, :rows], head[...].astype(bf16))

    loads["inv"].wait()
    loads["q1"].wait()
    loads["skip1"].wait()
    acc[...] = jnp.zeros_like(acc)

    @pl.loop(0, chunks)
    def _(c):
        cols = wide(c)

        @pl.when(me > 0)
        def _():
            border(c).wait_recv()

        spec = spectral_product(mm(fwd[...], win[c]), h1[c])
        short = mm(inv[rows:, :], spec)
        own = win[c, rows:, :].astype(f32)
        act = (q1[:, cols].astype(f32) * (short + skip1[:, cols] * own)).astype(bf16)
        weight_load(w1h, w1, w1_sem, c).wait()
        acc[...] += mm(act, w1[cols, :])

    loads["k2"].wait()
    loads["skip2"].wait()

    def ends_copy(o):
        return pltpu.make_async_remote_copy(
            src_ref=ends.at[o], dst_ref=got.at[me], send_sem=esend.at[o], recv_sem=erecv.at[me],
            device_id=place(o), device_id_type=MESH,
        )

    @pl.loop(0, chunks)
    def _(i):
        c = lax.rem(i + me, chunks)
        cols = wide(c)
        gated = (k2[:, cols].astype(f32) * acc[:, cols].astype(bf16).astype(f32)).astype(bf16)
        g2[c] = gated
        for j in range(WIDE // LANES):
            b = c * (WIDE // LANES) + j
            g = gated[:, j * LANES : (j + 1) * LANES].astype(f32)
            decay = a8[b]
            h = jnp.broadcast_to(g[:SUB][None], (modes, SUB, LANES))
            for m in range(1, rows // SUB):
                h = h * decay + g[m * SUB : (m + 1) * SUB][None]
            e = jnp.sum(h * p7[b], axis=1)
            for hi in range(modes // SUB):
                for s in range(per_tile):
                    o = (hi * blocks + b) * per_tile + s
                    piece = e[hi * SUB + s * part : hi * SUB + (s + 1) * part]
                    ends[o] = piece

                    @pl.when(o != me)
                    def _():
                        ends_copy(o).start()

                    @pl.when(o == me)
                    def _():
                        got[me] = piece

    @pl.loop(0, chunks)
    def _(c):
        gated = g2[c]
        spec = spectral_product(mm(fwd[:, :rows], gated), h2[c])
        y[c] = mm(inv[:rows, :], spec) + skip2[:, wide(c)] * gated.astype(f32)

    @pl.loop(0, n)
    def _(d):
        @pl.when(d != me)
        def _():
            pltpu.make_async_remote_copy(
                src_ref=ends.at[d], dst_ref=got.at[d], send_sem=esend.at[d], recv_sem=erecv.at[d],
                device_id=place(d), device_id_type=MESH,
            ).wait_recv()

    own_decay = jnp.exp(-float(rows) * tiled_rate[me])

    def scan(d, state):
        sout[d] = state
        return state * own_decay + got[d]

    lax.fori_loop(0, n, scan, jnp.zeros((part, LANES), f32))

    def state_copy(d):
        return pltpu.make_async_remote_copy(
            src_ref=sout.at[d], dst_ref=sin.at[me], send_sem=ssend.at[d], recv_sem=srecv.at[me],
            device_id=place(d), device_id_type=MESH,
        )

    @pl.loop(1, n)
    def _(p):
        state_copy(lax.rem(me + p, n)).start()

    sin[me] = sout[me]
    loads["q2"].wait()

    @pl.loop(0, n)
    def _(d):
        @pl.when(d != me)
        def _():
            pltpu.make_async_remote_copy(
                src_ref=sout.at[d], dst_ref=sin.at[d], send_sem=ssend.at[d], recv_sem=srecv.at[d],
                device_id=place(d), device_id_type=MESH,
            ).wait_recv()

    acc[...] = jnp.zeros_like(acc)

    @pl.loop(0, chunks)
    def _(c):
        cols = wide(c)
        for j in range(WIDE // LANES):
            b = c * (WIDE // LANES) + j
            lane = slice(j * LANES, (j + 1) * LANES)
            state = []
            for r in range(modes):
                hi, low = divmod(r, SUB)
                s, row = divmod(low, part)
                o = (hi * blocks + b) * per_tile + s
                state.append(jnp.broadcast_to(sin[o, row : row + 1, :], (SUB, LANES)))
            u = p1[b] * jnp.stack(state)
            decay = a8[b]
            for m in range(rows // SUB):
                span = slice(m * SUB, (m + 1) * SUB)
                head[span, lane] = jnp.sum(u, axis=0)
                u = u * decay
        act = (q2[:, cols].astype(f32) * (y[c] + head[...])).astype(bf16)
        weight_load(w2h, w2, w2_sem, c).wait()
        acc[...] += mm(act, w2[cols, :])

    out[...] = acc[...].astype(bf16)

    @pl.when(me < n - 1)
    def _():
        @pl.loop(0, chunks)
        def _(c):
            border(c).wait_send()

    @pl.loop(0, n)
    def _(d):
        @pl.when(d != me)
        def _():
            ends_copy(d).wait_send()
            state_copy(d).wait_send()


def local(q1, k1, v1, taps, skip1, w1, q2, k2, residue, rate, skip2, w2):
    rows, channels = q1.shape
    modes = rate.shape[0]
    minor = lax.axis_size("seqmin")
    n = lax.axis_size("seqmaj") * minor
    fwd, inv = dft_tables(rows)
    operands = (q1, k1, v1, taps, skip1[None], w1, q2, k2, residue, rate, skip2[None], w2, fwd, inv)
    chunks, blocks = channels // WIDE, channels // LANES
    states = (n, modes * channels // (n * LANES), LANES)
    scratch = [pltpu.VMEM(a.shape, a.dtype) for a in operands] + [
        pltpu.VMEM((chunks, 2 * rows, WIDE), bf16),
        pltpu.VMEM((chunks, 2 * rows, WIDE), f32),
        pltpu.VMEM((chunks, 2 * rows, WIDE), f32),
        pltpu.VMEM((blocks, modes, SUB, LANES), f32),
        pltpu.VMEM((blocks, modes, SUB, LANES), f32),
        pltpu.VMEM((blocks, modes, SUB, LANES), f32),
        pltpu.VMEM((rows, WIDE), f32),
        pltpu.VMEM((rows, channels), f32),
        pltpu.VMEM((chunks, rows, WIDE), f32),
        pltpu.VMEM((chunks, rows, WIDE), bf16),
        pltpu.VMEM(states, f32),
        pltpu.VMEM(states, f32),
        pltpu.VMEM(states, f32),
        pltpu.VMEM(states, f32),
        pltpu.VMEM(states, f32),
        pltpu.SemaphoreType.DMA((12,)),
        pltpu.SemaphoreType.DMA((chunks,)),
        pltpu.SemaphoreType.DMA((chunks,)),
        pltpu.SemaphoreType.DMA((chunks,)),
        pltpu.SemaphoreType.DMA((chunks,)),
        pltpu.SemaphoreType.DMA((n,)),
        pltpu.SemaphoreType.DMA((n,)),
        pltpu.SemaphoreType.DMA((n,)),
        pltpu.SemaphoreType.DMA((n,)),
    ]
    return pl.pallas_call(
        functools.partial(kernel, n, minor),
        out_shape=jax.ShapeDtypeStruct((rows, channels), bf16),
        in_specs=[pl.BlockSpec(memory_space=pl.ANY)] * len(operands),
        out_specs=pl.BlockSpec(memory_space=pltpu.VMEM),
        scratch_shapes=scratch,
        compiler_params=pltpu.CompilerParams(
            collective_id=0, has_side_effects=True, vmem_limit_bytes=48 * 1024 * 1024
        ),
    )(*operands)


def solution(mesh):
    s, r = P(axes, None), P()
    specs = (s, s, s, r, r, r, s, s, r, r, r, r)
    return jax.shard_map(local, mesh=mesh, in_specs=specs, out_specs=s, check_vma=False)
```

time: 81 us -> 46.7 us (0.58)
  Pallas kernels: 0 us -> 34.1 us
  matrix products: 29.4 us -> 0 us
  other arithmetic: 24 us -> 0 us
  starting transfers between devices: 12.4 us -> 0 us
  waiting for transfers between devices: 8.46 us -> 0 us
  local copies, waits for them, and re-layouts: 5.98 us -> 12 us
    pallas_call x0 -> x1, Pallas kernels: none -> 34.1 us  [local(): pl.pallas_call(functools.partial(kernel, n, minor), out_shape=jax.ShapeDt...]
    dot_general x9 -> x0, matrix products: 29.4 us -> none  [the longest x7 14.6 us: mm(): jnp.dot(a.astype(jnp.bfloat16), b.astype(jnp.bfloat16), preferred_element...]
    reduce_sum x3 -> x0, other arithmetic: 18.6 us -> none  [the longest x1 9.9 us: local(): head = jnp.sum(weight[None] * powers, axis=1)]
    all_to_all x2 -> x0, starting transfers between devices: 9.85 us -> none  [the longest x1 7.1 us: local(): lax.all_to_all(ends.reshape(n, flat).astype(bf16), axes, 0, 0, tiled=True)]
    all_to_all x2 -> x0, waiting for transfers between devices: 8.46 us -> none  [the longest x1 4.3 us: local(): lax.all_to_all(carry.astype(bf16), axes, 0, 0, tiled=True).astype(f32)]
    unnamed x38 -> x25, local copies, waits for them, and re-layouts: 5.24 us -> 12 us
    ppermute x1 -> x0, starting transfers between devices: 2.53 us -> none  [local(): border = lax.ppermute(g1, axes, [(i, i + 1) for i in range(n - 1)])]
    convert_element_type x4 -> x0, other arithmetic: 2.22 us -> none  [the longest x1 1.04 us: local(): ends.reshape(n, flat).astype(bf16)]
  transfers between devices with their start and end apart: 3 -> 0, of which waited for: 2 -> 0; matrix products, arithmetic and copies ran while one was open for 18% -> 0% of each run, Pallas kernels for 0% -> 0%
where the time goes in v2:
time: 46.7 us; the launch traced here: 46.2 us
  Pallas kernels  34.1 us (73%)
  local copies, waits for them, and re-layouts  12 us (26%)
    pallas_call x1, Pallas kernels, local(): pl.pallas_call(functools.partial(kernel, n, minor), out_shape=jax.ShapeDt...  34.1 us
    unnamed x25, local copies, waits for them, and re-layouts  12 us

profile of v2, /device:TPU:0, one launch (start us, length us, event | category | flops | bytes accessed | tf_op | source)
XLA Modules:
  0.0 46.2 jit_solution(5936948591098459808)
XLA Ops:
  0.0 1.0 %copy-done = bf16[128,2048]{1,0:T(8,128)(2,1)S(1)} copy-done((bf16[128,2048]{1,0:T(8,128)(2,1)S(1)}, bf16[128,2048]{1,0:T(8,128)(2,1)}, u32[]{:S(2)}) %copy-start) | copy-done | bytes 524312
  1.0 0.0 copy-start.1
  1.0 1.0 %copy-done.1 = bf16[128,2048]{1,0:T(8,128)(2,1)S(1)} copy-done((bf16[128,2048]{1,0:T(8,128)(2,1)S(1)}, bf16[128,2048]{1,0:T(8,128)(2,1)}, u32[]{:S(2)}) %copy-start.1) | copy-done | bytes 524312
  2.1 0.0 copy-start.2
  2.1 1.0 %copy-done.2 = bf16[128,2048]{1,0:T(8,128)(2,1)S(1)} copy-done((bf16[128,2048]{1,0:T(8,128)(2,1)S(1)}, bf16[128,2048]{1,0:T(8,128)(2,1)}, u32[]{:S(2)}) %copy-start.2) | copy-done | bytes 524312
  3.1 0.0 copy-start.3
  3.1 1.0 %copy-done.3 = bf16[128,2048]{1,0:T(8,128)(2,1)S(1)} copy-done((bf16[128,2048]{1,0:T(8,128)(2,1)S(1)}, bf16[128,2048]{1,0:T(8,128)(2,1)}, u32[]{:S(2)}) %copy-start.3) | copy-done | bytes 524312
  4.2 0.0 copy-start.4
  4.2 1.0 %copy-done.4 = bf16[128,2048]{1,0:T(8,128)(2,1)S(1)} copy-done((bf16[128,2048]{1,0:T(8,128)(2,1)S(1)}, bf16[128,2048]{1,0:T(8,128)(2,1)}, u32[]{:S(2)}) %copy-start.4) | copy-done | bytes 524312
  5.2 0.0 copy-start.5
  5.2 1.0 %copy-done.5 = bf16[128,2048]{1,0:T(8,128)(2,1)S(1)} copy-done((bf16[128,2048]{1,0:T(8,128)(2,1)S(1)}, bf16[128,2048]{1,0:T(8,128)(2,1)}, u32[]{:S(2)}) %copy-start.5) | copy-done | bytes 524312
  6.3 0.0 copy-start.6
  6.3 0.9 %copy-done.6 = f32[16,2048]{1,0:T(8,128)S(1)} copy-done((f32[16,2048]{1,0:T(8,128)S(1)}, f32[16,2048]{1,0:T(8,128)}, u32[]{:S(2)}) %copy-start.6) | copy-done | bytes 131096
  7.2 0.0 copy-start.7
  7.2 0.9 %copy-done.7 = f32[16,2048]{1,0:T(8,128)S(1)} copy-done((f32[16,2048]{1,0:T(8,128)S(1)}, f32[16,2048]{1,0:T(8,128)}, u32[]{:S(2)}) %copy-start.7) | copy-done | bytes 131096
  8.1 0.0 copy-start.8
  8.1 0.9 %copy-done.8 = bf16[256,256]{1,0:T(8,128)(2,1)S(1)} copy-done((bf16[256,256]{1,0:T(8,128)(2,1)S(1)}, bf16[256,256]{1,0:T(8,128)(2,1)}, u32[]{:S(2)}) %copy-start.8) | copy-done | bytes 131096
  9.0 0.0 copy-start.9
  9.0 0.9 %copy-done.9 = bf16[256,256]{1,0:T(8,128)(2,1)S(1)} copy-done((bf16[256,256]{1,0:T(8,128)(2,1)S(1)}, bf16[256,256]{1,0:T(8,128)(2,1)}, u32[]{:S(2)}) %copy-start.9) | copy-done | bytes 131096
  9.9 0.0 copy-start.10
  9.9 0.7 %copy-done.10 = f32[2048]{0:T(1024)S(1)} copy-done((f32[2048]{0:T(1024)S(1)}, f32[2048]{0:T(1024)}, u32[]{:S(2)}) %copy-start.10) | copy-done | bytes 8216
  10.6 0.7 %copy-done.11 = f32[2048]{0:T(1024)S(1)} copy-done((f32[2048]{0:T(1024)S(1)}, f32[2048]{0:T(1024)}, u32[]{:S(2)}) %copy-start.11) | copy-done | bytes 8216
  11.3 34.1 %shard_map.136 = bf16[128,2048]{1,0:T(8,128)(2,1)S(1)} custom-call(bf16[128,2048]{1,0:T(8,128)(2,1)S(1)} %copy-done, bf16[128,2048]{1,0:T(8,128)(2,1)S(1)} %copy-done.1, bf16[128,2048]{1,0:T(8,128)(2,1)S(1)} %copy-done.2, bf16[128,2048]{1,0:T(8,128)(2,1)S(1)} %copy-done.3, f32[1,2048]{1,0:T(1,128)S(1)} %bitcast.2, bf16[2048,2048]{1,0:T(8,128)(2,1)} %w1h.1, ...), custom_call_target="tpu_custom_call" | custom-call | tf_op jit(solution)/shard_map/pallas_call | solution.py:326
  45.4 0.8 %copy.16 = bf16[128,2048]{1,0:T(8,128)(2,1)} copy(bf16[128,2048]{1,0:T(8,128)(2,1)S(1)} %shard_map.136) | data formatting | bytes 1048576
  (2 shorter events, 0.0 us)
Async XLA Ops:
  0.0 1.0 %copy-start = (bf16[128,2048]{1,0:T(8,128)(2,1)S(1)}, bf16[128,2048]{1,0:T(8,128)(2,1)}, u32[]{:S(2)}) copy-start(bf16[128,2048]{1,0:T(8,128)(2,1)} %q1h.1) | copy-start | bytes 1572868
  1.0 1.0 %copy-start.1 = (bf16[128,2048]{1,0:T(8,128)(2,1)S(1)}, bf16[128,2048]{1,0:T(8,128)(2,1)}, u32[]{:S(2)}) copy-start(bf16[128,2048]{1,0:T(8,128)(2,1)} %k1h.1) | copy-start | bytes 1572868
  2.1 1.0 %copy-start.2 = (bf16[128,2048]{1,0:T(8,128)(2,1)S(1)}, bf16[128,2048]{1,0:T(8,128)(2,1)}, u32[]{:S(2)}) copy-start(bf16[128,2048]{1,0:T(8,128)(2,1)} %v1h.1) | copy-start | bytes 1572868
  3.1 1.0 %copy-start.3 = (bf16[128,2048]{1,0:T(8,128)(2,1)S(1)}, bf16[128,2048]{1,0:T(8,128)(2,1)}, u32[]{:S(2)}) copy-start(bf16[128,2048]{1,0:T(8,128)(2,1)} %tapsh.1) | copy-start | bytes 1572868
  4.2 1.0 %copy-start.4 = (bf16[128,2048]{1,0:T(8,128)(2,1)S(1)}, bf16[128,2048]{1,0:T(8,128)(2,1)}, u32[]{:S(2)}) copy-start(bf16[128,2048]{1,0:T(8,128)(2,1)} %q2h.1) | copy-start | bytes 1572868
  5.2 1.0 %copy-start.5 = (bf16[128,2048]{1,0:T(8,128)(2,1)S(1)}, bf16[128,2048]{1,0:T(8,128)(2,1)}, u32[]{:S(2)}) copy-start(bf16[128,2048]{1,0:T(8,128)(2,1)} %k2h.1) | copy-start | bytes 1572868
  6.3 0.9 %copy-start.6 = (f32[16,2048]{1,0:T(8,128)S(1)}, f32[16,2048]{1,0:T(8,128)}, u32[]{:S(2)}) copy-start(f32[16,2048]{1,0:T(8,128)} %resh.1) | copy-start | bytes 393220
  7.2 0.9 %copy-start.7 = (f32[16,2048]{1,0:T(8,128)S(1)}, f32[16,2048]{1,0:T(8,128)}, u32[]{:S(2)}) copy-start(f32[16,2048]{1,0:T(8,128)} %rateh.1) | copy-start | bytes 393220
  8.1 0.9 %copy-start.8 = (bf16[256,256]{1,0:T(8,128)(2,1)S(1)}, bf16[256,256]{1,0:T(8,128)(2,1)}, u32[]{:S(2)}) copy-start(bf16[256,256]{1,0:T(8,128)(2,1)} %constant.5.clone.invh) | copy-start | bytes 393220
  9.0 0.9 %copy-start.9 = (bf16[256,256]{1,0:T(8,128)(2,1)S(1)}, bf16[256,256]{1,0:T(8,128)(2,1)}, u32[]{:S(2)}) copy-start(bf16[256,256]{1,0:T(8,128)(2,1)} %constant.4.clone.fwdh) | copy-start | bytes 393220
  9.9 0.7 %copy-start.10 = (f32[2048]{0:T(1024)S(1)}, f32[2048]{0:T(1024)}, u32[]{:S(2)}) copy-start(f32[2048]{0:T(1024)} %param.18) | copy-start | bytes 24580
  10.6 0.7 %copy-start.11 = (f32[2048]{0:T(1024)S(1)}, f32[2048]{0:T(1024)}, u32[]{:S(2)}) copy-start(f32[2048]{0:T(1024)} %param.24) | copy-start | bytes 24580

commit v3 on v2

--- a/solution.py
+++ b/solution.py
@@ -326,11 +326,11 @@
     return pl.pallas_call(
         functools.partial(kernel, n, minor),
         out_shape=jax.ShapeDtypeStruct((rows, channels), bf16),
-        in_specs=[pl.BlockSpec(memory_space=pl.ANY)] * len(operands),
+        in_specs=[pl.BlockSpec(memory_space=pltpu.HBM)] * len(operands),
         out_specs=pl.BlockSpec(memory_space=pltpu.VMEM),
         scratch_shapes=scratch,
         compiler_params=pltpu.CompilerParams(
-            collective_id=0, has_side_effects=True, vmem_limit_bytes=48 * 1024 * 1024
+            collective_id=0, has_side_effects=True, vmem_limit_bytes=60 * 1024 * 1024
         ),
     )(*operands)
 

time: 46.7 us -> 36.1 us (0.77)
  local copies, waits for them, and re-layouts: 12 us -> 1.88 us
    unnamed x25 -> x1, local copies, waits for them, and re-layouts: 12 us -> 1.88 us
where the time goes in v3:
time: 36.1 us; the launch traced here: 35.9 us
  Pallas kernels  34 us (94%)
  local copies, waits for them, and re-layouts  1.88 us (5%)
    pallas_call x1, Pallas kernels, local(): pl.pallas_call(functools.partial(kernel, n, minor), out_shape=jax.ShapeDt...  34 us
    unnamed x1, local copies, waits for them, and re-layouts  1.88 us

profile of v3, /device:TPU:0, one launch (start us, length us, event | category | flops | bytes accessed | tf_op | source)
XLA Modules:
  0.0 35.9 jit_solution(8520492529242205831)
XLA Ops:
  0.0 34.0 %shard_map.136 = bf16[128,2048]{1,0:T(8,128)(2,1)} custom-call(bf16[128,2048]{1,0:T(8,128)(2,1)} %q1h.1, bf16[128,2048]{1,0:T(8,128)(2,1)} %k1h.1, bf16[128,2048]{1,0:T(8,128)(2,1)} %v1h.1, bf16[128,2048]{1,0:T(8,128)(2,1)} %tapsh.1, f32[1,2048]{1,0:T(1,128)} %bitcast.2, bf16[2048,2048]{1,0:T(8,128)(2,1)} %w1h.1, bf16[128,2048]{1,0:T(8,128)(2,1)} %q2h.1, ...), custom_call_target="tpu_custom_call" | custom-call | tf_op jit(solution)/shard_map/pallas_call | solution.py:326
  34.0 1.9 %copy.16 = bf16[128,2048]{1,0:T(8,128)(2,1)} copy(bf16[128,2048]{1,0:T(8,128)(2,1)} %shard_map.136) | data formatting | bytes 1048576

commit v4 on v3

--- a/solution.py
+++ b/solution.py
@@ -11,7 +11,7 @@
 axes = ("seqmaj", "seqmin")
 MESH = pl.DeviceIdType.MESH
 f32, bf16 = jnp.float32, jnp.bfloat16
-WIDE = 256
+WIDE = 512
 LANES = 128
 SUB = 8
 

time: 36.1 us -> 34.8 us (0.964)
  Pallas kernels: 34 us -> 32.7 us
    pallas_call x1, Pallas kernels: 34 us -> 32.7 us  [local(): pl.pallas_call(functools.partial(kernel, n, minor), out_shape=jax.ShapeDt...]
where the time goes in v4:
time: 34.8 us; the launch traced here: 34.6 us
  Pallas kernels  32.7 us (94%)
  local copies, waits for them, and re-layouts  1.88 us (5%)
    pallas_call x1, Pallas kernels, local(): pl.pallas_call(functools.partial(kernel, n, minor), out_shape=jax.ShapeDt...  32.7 us
    unnamed x1, local copies, waits for them, and re-layouts  1.88 us

profile of v4, /device:TPU:0, one launch (start us, length us, event | category | flops | bytes accessed | tf_op | source)
XLA Modules:
  0.0 34.6 jit_solution(14519386572894474603)
XLA Ops:
  0.0 32.7 %shard_map.136 = bf16[128,2048]{1,0:T(8,128)(2,1)} custom-call(bf16[128,2048]{1,0:T(8,128)(2,1)} %q1h.1, bf16[128,2048]{1,0:T(8,128)(2,1)} %k1h.1, bf16[128,2048]{1,0:T(8,128)(2,1)} %v1h.1, bf16[128,2048]{1,0:T(8,128)(2,1)} %tapsh.1, f32[1,2048]{1,0:T(1,128)} %bitcast.2, bf16[2048,2048]{1,0:T(8,128)(2,1)} %w1h.1, bf16[128,2048]{1,0:T(8,128)(2,1)} %q2h.1, ...), custom_call_target="tpu_custom_call" | custom-call | tf_op jit(solution)/shard_map/pallas_call | solution.py:326
  32.7 1.9 %copy.16 = bf16[128,2048]{1,0:T(8,128)(2,1)} copy(bf16[128,2048]{1,0:T(8,128)(2,1)} %shard_map.136) | data formatting | bytes 1048576

commit v5 on v4

--- a/solution.py
+++ b/solution.py
@@ -169,9 +169,16 @@
     loads["k2"].wait()
     loads["skip2"].wait()
 
+    def all_tiles(src, dst, send_sem, recv_sem):
+        others = pl.ds(0, n - 1)
+        return pltpu.make_async_remote_copy(
+            src_ref=src.at[others], dst_ref=dst.at[others], send_sem=send_sem.at[0], recv_sem=recv_sem.at[0],
+            device_id=place(lax.rem(me + 1, n)), device_id_type=MESH,
+        )
+
     def ends_copy(o):
         return pltpu.make_async_remote_copy(
-            src_ref=ends.at[o], dst_ref=got.at[me], send_sem=esend.at[o], recv_sem=erecv.at[me],
+            src_ref=ends.at[o], dst_ref=got.at[me], send_sem=esend.at[0], recv_sem=erecv.at[0],
             device_id=place(o), device_id_type=MESH,
         )
 
@@ -209,14 +216,7 @@
         spec = spectral_product(mm(fwd[:, :rows], gated), h2[c])
         y[c] = mm(inv[:rows, :], spec) + skip2[:, wide(c)] * gated.astype(f32)
 
-    @pl.loop(0, n)
-    def _(d):
-        @pl.when(d != me)
-        def _():
-            pltpu.make_async_remote_copy(
-                src_ref=ends.at[d], dst_ref=got.at[d], send_sem=esend.at[d], recv_sem=erecv.at[d],
-                device_id=place(d), device_id_type=MESH,
-            ).wait_recv()
+    all_tiles(ends, got, esend, erecv).wait_recv()
 
     own_decay = jnp.exp(-float(rows) * tiled_rate[me])
 
@@ -228,7 +228,7 @@
 
     def state_copy(d):
         return pltpu.make_async_remote_copy(
-            src_ref=sout.at[d], dst_ref=sin.at[me], send_sem=ssend.at[d], recv_sem=srecv.at[me],
+            src_ref=sout.at[d], dst_ref=sin.at[me], send_sem=ssend.at[0], recv_sem=srecv.at[0],
             device_id=place(d), device_id_type=MESH,
         )
 
@@ -239,14 +239,7 @@
     sin[me] = sout[me]
     loads["q2"].wait()
 
-    @pl.loop(0, n)
-    def _(d):
-        @pl.when(d != me)
-        def _():
-            pltpu.make_async_remote_copy(
-                src_ref=sout.at[d], dst_ref=sin.at[d], send_sem=ssend.at[d], recv_sem=srecv.at[d],
-                device_id=place(d), device_id_type=MESH,
-            ).wait_recv()
+    all_tiles(sout, sin, ssend, srecv).wait_recv()
 
     acc[...] = jnp.zeros_like(acc)
 
@@ -280,12 +273,8 @@
         def _(c):
             border(c).wait_send()
 
-    @pl.loop(0, n)
-    def _(d):
-        @pl.when(d != me)
-        def _():
-            ends_copy(d).wait_send()
-            state_copy(d).wait_send()
+    all_tiles(ends, got, esend, erecv).wait_send()
+    all_tiles(sout, sin, ssend, srecv).wait_send()
 
 
 def local(q1, k1, v1, taps, skip1, w1, q2, k2, residue, rate, skip2, w2):
@@ -318,10 +307,10 @@
         pltpu.SemaphoreType.DMA((chunks,)),
         pltpu.SemaphoreType.DMA((chunks,)),
         pltpu.SemaphoreType.DMA((chunks,)),
-        pltpu.SemaphoreType.DMA((n,)),
-        pltpu.SemaphoreType.DMA((n,)),
-        pltpu.SemaphoreType.DMA((n,)),
-        pltpu.SemaphoreType.DMA((n,)),
+        pltpu.SemaphoreType.DMA((1,)),
+        pltpu.SemaphoreType.DMA((1,)),
+        pltpu.SemaphoreType.DMA((1,)),
+        pltpu.SemaphoreType.DMA((1,)),
     ]
     return pl.pallas_call(
         functools.partial(kernel, n, minor),

time: 34.8 us -> 33.3 us (0.957)
  Pallas kernels: 32.7 us -> 31.2 us
    pallas_call x1, Pallas kernels: 32.7 us -> 31.2 us  [local(): pl.pallas_call(functools.partial(kernel, n, minor), out_shape=jax.ShapeDt...]
where the time goes in v5:
time: 33.3 us; the launch traced here: 33.1 us
  Pallas kernels  31.2 us (94%)
  local copies, waits for them, and re-layouts  1.88 us (6%)
    pallas_call x1, Pallas kernels, local(): pl.pallas_call(functools.partial(kernel, n, minor), out_shape=jax.ShapeDt...  31.2 us
    unnamed x1, local copies, waits for them, and re-layouts  1.88 us

profile of v5, /device:TPU:0, one launch (start us, length us, event | category | flops | bytes accessed | tf_op | source)
XLA Modules:
  0.0 33.1 jit_solution(15316698258935948857)
XLA Ops:
  0.0 31.2 %shard_map.136 = bf16[128,2048]{1,0:T(8,128)(2,1)} custom-call(bf16[128,2048]{1,0:T(8,128)(2,1)} %q1h.1, bf16[128,2048]{1,0:T(8,128)(2,1)} %k1h.1, bf16[128,2048]{1,0:T(8,128)(2,1)} %v1h.1, bf16[128,2048]{1,0:T(8,128)(2,1)} %tapsh.1, f32[1,2048]{1,0:T(1,128)} %bitcast.2, bf16[2048,2048]{1,0:T(8,128)(2,1)} %w1h.1, bf16[128,2048]{1,0:T(8,128)(2,1)} %q2h.1, ...), custom_call_target="tpu_custom_call" | custom-call | tf_op jit(solution)/shard_map/pallas_call | solution.py:315
  31.3 1.9 %copy.16 = bf16[128,2048]{1,0:T(8,128)(2,1)} copy(bf16[128,2048]{1,0:T(8,128)(2,1)} %shard_map.136) | data formatting | bytes 1048576
